TPU v7x, 32 devices: a whole 2x2x4 slice. The times are simulated.
32 devices in a mesh: row: 16 (over z, y, x), rep: 2 (over core).
Axes of the slice: x: 2, y: 2, z: 4, core: 2. Of those that a mesh axis runs over, the one named last changes fastest.
Arguments:
- node_feats: bfloat16 [4096, 256], P(('row', 'rep')), may hold values from -6 to 6
- edge_feats: bfloat16 [32768, 256], P(('row', 'rep')), may hold values from -6 to 6
- senders: int32 [32768], P(('row', 'rep')), may hold values from 0 to 4095, as said below
- receivers: int32 [32768], P(('row', 'rep')), may hold values from 0 to 4095, as said below
- edge_count: int32 [32], P(('row', 'rep')), may hold values from 512 to 1024, as said below
- w_edge_in: bfloat16 [768, 256], replicated, may hold values from -0.21875 to 0.21875
- w_edge_out: bfloat16 [256, 256], replicated, may hold values from -0.375 to 0.375
- gain_edge: float32 [256], replicated, may hold values from 0.5 to 2
- w_node_in: bfloat16 [512, 256], replicated, may hold values from -0.25 to 0.25
- w_node_out: bfloat16 [256, 256], replicated, may hold values from -0.375 to 0.375
- gain_node: float32 [256], replicated, may hold values from 0.5 to 2
- d_nodes_out: bfloat16 [4096, 256], P(('row', 'rep')), may hold values from -6 to 6
- d_edges_out: bfloat16 [32768, 256], P(('row', 'rep')), may hold values from -6 to 6
Outputs:
- nodes_out: bfloat16 [4096, 256], P(('row', 'rep'))
- edges_out: bfloat16 [32768, 256], P(('row', 'rep'))
- d_nodes: bfloat16 [4096, 256], P(('row', 'rep'))
- d_edges: bfloat16 [32768, 256], P(('row', 'rep'))
- d_w_edge_in: bfloat16 [768, 256], replicated
- d_w_edge_out: bfloat16 [256, 256], replicated
- d_gain_edge: float32 [256], replicated
- d_w_node_in: bfloat16 [512, 256], replicated
- d_w_node_out: bfloat16 [256, 256], replicated
- d_gain_node: float32 [256], replicated
Inputs may be any that keep to these rules, and one draw needn't show every extreme that they name: `receivers`: edge i's receiver lies in nodes g * 256 to (g + 1) * 256 - 1 with g = i // 2048. `senders`: an edge's sender differs from its receiver by at most 128; in every aligned block of 1024 edge slots some edge reaches 128. The first edge_count[k] slots of the k-th aligned block of 1024 slots are live; some block is full.
All inputs are finite; a program needn't handle non-finite values.
Results may differ from a plain program's by a relative error of at most 0.013.
Values may be sent and summed in bfloat16 or wider, within the bound.
A program may use at most 64 MiB of HBM per device.

v0:
```python
import jax
import jax.numpy as jnp
from jax import lax
from jax.sharding import PartitionSpec as P


def padded(x, sides, width):
    for axis, dim in sides:
        devices, length = (lax.axis_size(axis), x.shape[dim])
        up = [(i, (i + 1) % devices) for i in range(devices - 1)]
        down = [(j, i) for i, j in up]
        last = lax.slice_in_dim(x, length - width, length, axis=dim)
        first = lax.slice_in_dim(x, 0, width, axis=dim)
        before = lax.ppermute(last, axis, up)
        after = lax.ppermute(first, axis, down)
        x = jnp.concatenate([before, x, after], axis=dim)
    return x


def from_behind(value, axis, steps):
    count = lax.axis_size(axis)
    first, last = (max(0, -steps), min(count, count - steps))
    return lax.ppermute(value, axis, [(source, source + steps) for source in range(first, last)])


def silu_slope(pre):
    sigmoid = jax.nn.sigmoid(pre)
    return sigmoid * (1.0 + pre * (1.0 - sigmoid))


def layer_norm(values):
    centred = values - jnp.mean(values, axis=-1, keepdims=True)
    inv_scale = lax.rsqrt(jnp.mean(centred * centred, axis=-1, keepdims=True) + 1e-05)
    return (centred * inv_scale, inv_scale)


def norm_back(upstream, normed, inv_scale):
    return inv_scale * (
        upstream
        - jnp.mean(upstream, axis=-1, keepdims=True)
        - normed * jnp.mean(upstream * normed, axis=-1, keepdims=True)
    )


def contract_rows(left, right):
    return lax.dot_general(
        left, right, (((0,), (0,)), ((), ())), preferred_element_type=jnp.float32
    )


def times_transpose(left, right):
    return lax.dot_general(
        left, right, (((1,), (1,)), ((), ())), preferred_element_type=jnp.float32
    )


def local(
    node_feats,
    edge_feats,
    senders,
    receivers,
    edge_count,
    w_edge_in,
    w_edge_out,
    gain_edge,
    w_node_in,
    w_node_out,
    gain_node,
    d_nodes_out,
    d_edges_out,
):
    width = node_feats.shape[1]
    edge_rows = edge_feats.shape[0]
    grouped = lax.all_gather(node_feats, "rep", axis=0, tiled=True)
    group_rows = grouped.shape[0]
    rim_rows = group_rows // 2
    extended = padded(grouped, (("row", 0),), rim_rows)
    group_start = lax.axis_index("row") * group_rows
    recv_local = receivers - group_start
    send_local = senders - group_start + rim_rows
    slots = jnp.arange(edge_rows, dtype=jnp.int32)
    live_mask = (slots < edge_count[0]).astype(jnp.float32)[:, None]
    edge_input = jnp.concatenate(
        [edge_feats, jnp.take(extended, send_local, axis=0), jnp.take(grouped, recv_local, axis=0)],
        axis=1,
    )
    edge_pre = jnp.dot(edge_input, w_edge_in, preferred_element_type=jnp.float32)
    edge_act = jax.nn.silu(edge_pre).astype(jnp.bfloat16)
    edge_mix = jnp.dot(edge_act, w_edge_out, preferred_element_type=jnp.float32)
    edge_norm, edge_scale = layer_norm(edge_mix)
    message = live_mask * edge_norm * gain_edge
    edges_out = (edge_feats.astype(jnp.float32) + message).astype(jnp.bfloat16)
    message_b = message.astype(jnp.bfloat16)
    recv_table = (
        lax.broadcasted_iota(jnp.int32, (group_rows, edge_rows), 0) == recv_local[None, :]
    ).astype(jnp.bfloat16)
    partial_sums = jnp.dot(recv_table, message_b, preferred_element_type=jnp.float32)
    aggregate = lax.psum_scatter(partial_sums, "rep", scatter_dimension=0, tiled=True)
    node_input = jnp.concatenate([node_feats, aggregate.astype(jnp.bfloat16)], axis=1)
    node_pre = jnp.dot(node_input, w_node_in, preferred_element_type=jnp.float32)
    node_act = jax.nn.silu(node_pre).astype(jnp.bfloat16)
    node_mix = jnp.dot(node_act, w_node_out, preferred_element_type=jnp.float32)
    node_norm, node_scale = layer_norm(node_mix)
    nodes_out = (node_feats.astype(jnp.float32) + node_norm * gain_node).astype(jnp.bfloat16)
    grad_nodes = d_nodes_out.astype(jnp.float32)
    d_gain_node = jnp.sum(grad_nodes * node_norm, axis=0)
    d_node_mix = norm_back(grad_nodes * gain_node, node_norm, node_scale).astype(jnp.bfloat16)
    d_w_node_out = contract_rows(node_act, d_node_mix)
    d_node_pre = (times_transpose(d_node_mix, w_node_out) * silu_slope(node_pre)).astype(
        jnp.bfloat16
    )
    d_w_node_in = contract_rows(node_input, d_node_pre)
    d_node_input = times_transpose(d_node_pre, w_node_in)
    d_aggregate = d_node_input[:, width:].astype(jnp.bfloat16)
    d_direct = grad_nodes + d_node_input[:, :width]
    group_grad = lax.all_gather(d_aggregate, "rep", axis=0, tiled=True)
    d_message = live_mask * (
        d_edges_out.astype(jnp.float32)
        + jnp.take(group_grad, recv_local, axis=0).astype(jnp.float32)
    )
    d_gain_edge = jnp.sum(d_message * edge_norm, axis=0)
    d_edge_mix = norm_back(d_message * gain_edge, edge_norm, edge_scale).astype(jnp.bfloat16)
    d_w_edge_out = contract_rows(edge_act, d_edge_mix)
    d_edge_pre = (times_transpose(d_edge_mix, w_edge_out) * silu_slope(edge_pre)).astype(
        jnp.bfloat16
    )
    d_w_edge_in = contract_rows(edge_input, d_edge_pre)
    d_edge_input = times_transpose(d_edge_pre, w_edge_in)
    d_edges = (d_edges_out.astype(jnp.float32) + d_edge_input[:, :width]).astype(jnp.bfloat16)
    d_sender = d_edge_input[:, width : 2 * width].astype(jnp.bfloat16)
    d_receiver = d_edge_input[:, 2 * width :].astype(jnp.bfloat16)
    send_table = (
        lax.broadcasted_iota(jnp.int32, (group_rows + 2 * rim_rows, edge_rows), 0)
        == send_local[None, :]
    ).astype(jnp.bfloat16)
    send_sums = jnp.dot(send_table, d_sender, preferred_element_type=jnp.float32)
    recv_sums = jnp.dot(recv_table, d_receiver, preferred_element_type=jnp.float32)
    from_next = from_behind(send_sums[:rim_rows].astype(jnp.bfloat16), "row", -1).astype(
        jnp.float32
    )
    from_prev = from_behind(
        send_sums[group_rows + rim_rows :].astype(jnp.bfloat16), "row", 1
    ).astype(jnp.float32)
    inner = send_sums[rim_rows : rim_rows + group_rows]
    inner = jnp.concatenate([inner[:rim_rows] + from_prev, inner[rim_rows:] + from_next], axis=0)
    edge_terms = lax.psum_scatter(
        inner.astype(jnp.bfloat16), "rep", scatter_dimension=0, tiled=True
    ).astype(jnp.float32) + lax.psum_scatter(
        recv_sums.astype(jnp.bfloat16), "rep", scatter_dimension=0, tiled=True
    ).astype(
        jnp.float32
    )
    d_nodes = (d_direct + edge_terms).astype(jnp.bfloat16)
    summed = lax.psum(
        (d_w_edge_in, d_w_edge_out, d_gain_edge, d_w_node_in, d_w_node_out, d_gain_node),
        ("row", "rep"),
    )
    return (
        nodes_out,
        edges_out,
        d_nodes,
        d_edges,
        summed[0].astype(jnp.bfloat16),
        summed[1].astype(jnp.bfloat16),
        summed[2],
        summed[3].astype(jnp.bfloat16),
        summed[4].astype(jnp.bfloat16),
        summed[5],
    )


def solution(mesh):
    return jax.shard_map(
        local,
        mesh=mesh,
        in_specs=(
            P(("row", "rep"), None),
            P(("row", "rep"), None),
            P(("row", "rep")),
            P(("row", "rep")),
            P(("row", "rep")),
            P(),
            P(),
            P(),
            P(),
            P(),
            P(),
            P(("row", "rep"), None),
            P(("row", "rep"), None),
        ),
        out_specs=(
            P(("row", "rep"), None),
            P(("row", "rep"), None),
            P(("row", "rep"), None),
            P(("row", "rep"), None),
            P(),
            P(),
            P(),
            P(),
            P(),
            P(),
        ),
        check_vma=False,
    )
```

profile of v0, /device:TPU:0, one launch (start us, length us, event | category | flops | bytes accessed | tf_op | source)
XLA Modules:
  0.0 151.7 jit_solution(1003866890800980398)
XLA Ops:
  7.2 2.4 %all_gather.6 = bf16[256,256]{1,0:T(8,128)(2,1)S(1)} all-gather(bf16[128,256]{1,0:T(8,128)(2,1)} %param.15), channel_id=1, replica_groups=mesh['row'=16,'rep'=2] {'rep'}, dimensions={0}, use_global_device_ids=true | all-gather | bytes 196608 | tf_op jit(solution)/shard_map/all_gather | solution.py:74
  9.6 4.7 %collective-permute-start = (bf16[128,256]{1,0:T(8,128)(2,1)S(1)}, bf16[128,256]{1,0:T(8,128)(2,1)S(1)}, u32[]{:S(2)}, u32[]{:S(2)}) collective-permute-start(bf16[128,256]{1,0:T(8,128)(2,1)S(1)} %get-tuple-element.42), channel_id=1, source_target_pairs={{0,2},{2,4},{4,6},{6,8},{8,10},{10,12},{12,14},{14,16},{16,18},{18... | collective-permute-start | bytes 196616 | tf_op jit(solution)/shard_map/ppermute | solution.py:14
  14.4 1.3 collective-permute-start.1
  16.4 1.3 subtract_add_fusion
  18.3 0.7 compare_and_fusion
  19.0 3.9 %gather_fusion.1 = bf16[1024,256]{1,0:T(8,128)(2,1)S(1)} fusion(bf16[256,256]{1,0:T(8,128)(2,1)S(1)} %all_gather.6, s32[1024]{0:T(1024)S(1)} %fusion.36), kind=kCustom, calls=%fused_computation.clone | custom fusion | bytes 1052672 | tf_op jit(solution)/shard_map/jit(_take)/gather | solution.py:84
  23.3 3.9 %gather_fusion = bf16[1024,256]{1,0:T(8,128)(2,1)S(1)} fusion(bf16[512,256]{1,0:T(8,128)(2,1)S(1)} %pad_maximum_fusion.3, s32[1024]{0:T(1024)S(1)} %get-tuple-element.45), kind=kCustom, calls=%fused_computation.2 | custom fusion | bytes 1052672 | tf_op jit(solution)/shard_map/jit(_take)/gather | solution.py:84
  27.5 1.6 %multiply_convert_fusion.1 = (bf16[1024,256]{1,0:T(8,128)(2,1)S(1)}, f32[1024,256]{1,0:T(8,128)}) fusion(bf16[768,256]{1,0:T(8,128)(2,1)S(1)} %copy-done, bf16[1024,256]{1,0:T(8,128)(2,1)S(1)} %broadcast_select_fusion, bf16[1024,256]{1,0:T(8,128)(2,1)S(1)} %broadcast_select_fusion.1, bf16[1024,256]{1,0:T(8,128)(2,1)S(1)} %copy-done.17), kind=kOutput, calls=%fused_computation.22 | convolution fusion | flops 408682496 | bytes 3538944 | tf_op jit(solution)/shard_map/dot_general | solution.py:87
  29.8 1.2 fusion.6
  31.0 1.0 copy.23
  32.3 9.0 %reduce-scatter.4.cloned.1.call-done = f32[128,256]{1,0:T(8,128)} async-done(((f32[256,256]{1,0:T(8,128)}), f32[128,256]{1,0:T(8,128)}) %reduce-scatter.4.cloned.1.call-update) | async-done | bytes 131088 | tf_op jit(solution)/shard_map/reduce_scatter | solution.py:98
  41.3 0.9 convert_element_type.98
  42.4 1.2 fusion.48
  43.8 1.3 fusion.30
  45.4 1.0 fusion.41
  47.3 1.9 %all_gather.7 = bf16[256,256]{1,0:T(8,128)(2,1)S(1)} all-gather(bf16[128,256]{1,0:T(8,128)(2,1)S(1)} %slice.81), channel_id=1, replica_groups=mesh['row'=16,'rep'=2] {'rep'}, dimensions={0}, use_global_device_ids=true | all-gather | bytes 196608 | tf_op jit(solution)/shard_map/all_gather | solution.py:116
  49.2 3.9 %gather_fusion.2 = bf16[1024,256]{1,0:T(8,128)(2,1)S(1)} fusion(bf16[256,256]{1,0:T(8,128)(2,1)S(1)} %all_gather.7, s32[1024]{0:T(1024)S(1)} %fusion.36), kind=kCustom, calls=%fused_computation.1.clone | custom fusion | bytes 1052672 | tf_op jit(solution)/shard_map/jit(_take)/gather | solution.py:119
  53.4 1.9 %multiply_reduce_fusion = (f32[256]{0:T(256)}, f32[1024]{0:T(1024)S(1)}, f32[1024]{0:T(1024)S(1)}) fusion(bf16[1024,256]{0,1:T(8,128)(2,1)S(1)} %copy.24, f32[1024,256]{0,1:T(8,128)S(1)} %get-tuple-element.49, f32[1024]{0:T(1024)S(1)} %add_rsqrt_fusion, f32[1024]{0:T(1024)S(1)} %broadcast_multiply_fusion.2, f32[1024]{0:T(1024)S(1)} %fusion.35, ...), kind=kLoop, calls=%fused_computation.15 | loop fusion | flops 3405568 | bytes 2120704 | tf_op jit(solution)/shard_map/reduce_sum | solution.py:121
  55.3 1.5 multiply_convert_fusion
  56.8 1.1 fusion.52
  59.2 1.5 fusion.10
  60.7 1.8 %fusion.49 = (bf16[1024,768]{1,0:T(8,128)(2,1)}, f32[1024,768]{1,0:T(8,128)S(1)}) fusion(bf16[1024,256]{1,0:T(8,128)(2,1)S(1)} %fusion.1, bf16[768,256]{1,0:T(8,128)(2,1)S(1)} %copy-done), kind=kOutput, calls=%fused_computation.99 | convolution fusion | flops 403439616 | bytes 5636096 | tf_op jit(solution)/shard_map/dot_general | solution.py:52
  63.6 2.0 %convolution_convert_fusion = bf16[256,256]{1,0:T(8,128)(2,1)} fusion(bf16[1024,768]{1,0:T(8,128)(2,1)} %get-tuple-element.52, s32[1024]{0:T(1024)S(1)} %copy-done.27), kind=kOutput, calls=%fused_computation.10 | convolution fusion | flops 134545408 | bytes 659456 | tf_op jit(solution)/shard_map/dot_general | solution.py:137
  65.6 2.4 %fusion.50 = (bf16[512,256]{1,0:T(8,128)(2,1)S(1)}, f32[512,256]{1,0:T(8,128)}) fusion(bf16[1024,768]{1,0:T(8,128)(2,1)} %get-tuple-element.52, s32[1024]{0:T(1024)S(1)} %copy-done.31), kind=kOutput, calls=%fused_computation.100 | convolution fusion | flops 269090816 | bytes 1314816 | tf_op jit(solution)/shard_map/dot_general | solution.py:136
  68.0 3.6 %collective-permute-start.2 = (bf16[128,256]{1,0:T(8,128)(2,1)S(1)}, bf16[128,256]{1,0:T(8,128)(2,1)S(1)}, u32[]{:S(2)}, u32[]{:S(2)}) collective-permute-start(bf16[128,256]{1,0:T(8,128)(2,1)S(1)} %get-tuple-element.39), channel_id=1, source_target_pairs={{0,2},{2,4},{4,6},{6,8},{8,10},{10,12},{12,14},{14,16},{16,18},{18... | collective-permute-start | bytes 196616 | tf_op jit(solution)/shard_map/ppermute | solution.py:23
  71.6 1.3 collective-permute-start.3
  73.2 1.0 copy.27
  74.2 1.0 copy.28
  75.3 2.4 %collective-permute-done.3 = bf16[128,256]{1,0:T(8,128)(2,1)S(1)} collective-permute-done((bf16[128,256]{1,0:T(8,128)(2,1)S(1)}, bf16[128,256]{1,0:T(8,128)(2,1)S(1)}, u32[]{:S(2)}, u32[]{:S(2)}) %collective-permute-start.3) | collective-permute-done | bytes 65568 | tf_op jit(solution)/shard_map/ppermute | solution.py:23
  77.7 1.0 fusion.32
  79.5 64.1 %all-reduce.2 = (bf16[768,256]{1,0:T(8,128)(2,1)}, bf16[256,256]{1,0:T(8,128)(2,1)}, f32[256]{0:T(256)}, bf16[512,256]{1,0:T(8,128)(2,1)}, bf16[256,256]{1,0:T(8,128)(2,1)}, /*index=5*/f32[256]{0:T(256)}) all-reduce(f32[768,256]{1,0:T(8,128)S(1)} %copy-done.9, ...), channel_id=1, replica_groups=mesh['row'=16,'rep'=2] {'row','rep'}, use_global_device_ids=true, to_apply=%region_11.13 | all-reduce | flops 459264 | bytes 2756608 | tf_op jit(solution)/shard_map/psum | solution.py:154
  143.6 1.5 %fusion.29 = bf16[128,256]{1,0:T(8,128)(2,1)} fusion(bf16[128,256]{1,0:T(8,128)(2,1)S(1)} %copy-done.21, f32[128,512]{1,0:T(8,128)S(1)} %copy-done.8, bf16[128,256]{1,0:T(8,128)(2,1)} %reduce-scatter.8.cloned.1.call-done, bf16[128,256]{1,0:T(8,128)(2,1)} %reduce-scatter.6.cloned.1.call-done), kind=kLoop, calls=%fused_computation.55 | loop fusion | flops 229376 | bytes 393216 | tf_op jit(solution)/shard_map/convert_element_type | solution.py:153
  (117 shorter events, 7.4 us)
Async XLA Ops:
  7.2 20.3 %copy-start = (bf16[768,256]{1,0:T(8,128)(2,1)S(1)}, bf16[768,256]{1,0:T(8,128)(2,1)}, u32[]{:S(2)}) copy-start(bf16[768,256]{1,0:T(8,128)(2,1)} %param.20) | copy-start | bytes 1179652
  7.2 34.1 %reduce-scatter.4.cloned.1.call-start = ((), (), s32[]{:S(2)}) async-start(), calls=%async_computation.3 | async-start | bytes 393216 | tf_op jit(solution)/shard_map/reduce_scatter | solution.py:98
  9.6 13.6 %collective-permute-start = (bf16[128,256]{1,0:T(8,128)(2,1)S(1)}, bf16[128,256]{1,0:T(8,128)(2,1)S(1)}, u32[]{:S(2)}, u32[]{:S(2)}) collective-permute-start(bf16[128,256]{1,0:T(8,128)(2,1)S(1)} %get-tuple-element.42), channel_id=1, source_target_pairs={{0,2},{2,4},{4,6},{6,8},{8,10},{10,12},{12,14},{14,16},{16,18},{18... | collective-permute-start | bytes 196616 | tf_op jit(solution)/shard_map/ppermute | solution.py:14
  14.4 8.9 %collective-permute-start.1 = (bf16[128,256]{1,0:T(8,128)(2,1)S(1)}, bf16[128,256]{1,0:T(8,128)(2,1)S(1)}, u32[]{:S(2)}, u32[]{:S(2)}) collective-permute-start(bf16[128,256]{1,0:T(8,128)(2,1)S(1)} %get-tuple-element.43), channel_id=1, source_target_pairs={{2,0},{4,2},{6,4},{8,6},{10,8},{12,10},{14,12},{16,14},{18,16},{20... | collective-permute-start | bytes 196616 | tf_op jit(solution)/shard_map/ppermute | solution.py:15
  19.0 4.0 %copy-start.28 = (pred[1024]{0:T(1024)(128)(4,1)}, pred[1024]{0:T(1024)(128)(4,1)S(1)}, u32[]{:S(2)}) copy-start(pred[1024]{0:T(1024)(128)(4,1)S(1)} %get-tuple-element.33) | copy-start | bytes 3076
  19.0 10.6 %copy-start.26 = (s32[1024]{0:T(1024)}, s32[1024]{0:T(1024)S(1)}, u32[]{:S(2)}) copy-start(s32[1024]{0:T(1024)S(1)} %get-tuple-element.34) | copy-start | bytes 12292
  23.2 4.2 %copy-start.12 = (bf16[1024,256]{1,0:T(8,128)(2,1)}, bf16[1024,256]{1,0:T(8,128)(2,1)S(1)}, u32[]{:S(2)}) copy-start(bf16[1024,256]{1,0:T(8,128)(2,1)S(1)} %broadcast_select_fusion) | copy-start | bytes 1572868
  23.3 4.2 %copy-start.17 = (bf16[1024,256]{1,0:T(8,128)(2,1)S(1)}, bf16[1024,256]{1,0:T(8,128)(2,1)}, u32[]{:S(2)}) copy-start(bf16[1024,256]{1,0:T(8,128)(2,1)} %param.16) | copy-start | bytes 1572868
  30.9 11.2 %copy-start.3 = (bf16[512,256]{1,0:T(8,128)(2,1)S(1)}, bf16[512,256]{1,0:T(8,128)(2,1)}, u32[]{:S(2)}) copy-start(bf16[512,256]{1,0:T(8,128)(2,1)} %param.23) | copy-start | bytes 786436
  30.9 11.3 %copy-start.5 = (bf16[128,256]{1,0:T(8,128)(2,1)S(1)}, bf16[128,256]{1,0:T(8,128)(2,1)}, u32[]{:S(2)}) copy-start(bf16[128,256]{1,0:T(8,128)(2,1)} %param.15) | copy-start | bytes 196612
  31.0 12.8 %copy-start.20 = (bf16[128,256]{1,0:T(8,128)(2,1)S(1)}, bf16[128,256]{1,0:T(8,128)(2,1)}, u32[]{:S(2)}) copy-start(bf16[128,256]{1,0:T(8,128)(2,1)} %param.26) | copy-start | bytes 196612
  31.0 12.8 %copy-start.35 = (f32[256]{0:T(256)S(1)}, f32[256]{0:T(256)}, u32[]{:S(2)}) copy-start(f32[256]{0:T(256)} %param.25) | copy-start | bytes 3076
  31.0 112.6 %reduce-scatter.8.cloned.1.call-start = ((), (), s32[]{:S(2)}) async-start(), calls=%async_computation.5 | async-start | bytes 196608 | tf_op jit(solution)/shard_map/reduce_scatter | solution.py:148
  32.2 12.9 %copy-start.36 = (bf16[256,256]{1,0:T(8,128)(2,1)S(1)}, bf16[256,256]{1,0:T(8,128)(2,1)}, u32[]{:S(2)}) copy-start(bf16[256,256]{1,0:T(8,128)(2,1)} %param.24) | copy-start | bytes 393220
  42.2 3.2 %copy-start.10 = (bf16[128,256]{1,0:T(8,128)(2,1)}, bf16[128,256]{1,0:T(8,128)(2,1)S(1)}, u32[]{:S(2)}) copy-start(bf16[128,256]{1,0:T(8,128)(2,1)S(1)} %convert_element_type.98) | copy-start | bytes 196612
  45.4 3.8 %copy-start.22 = (bf16[128,256]{1,0:T(8,128)(2,1)}, bf16[128,256]{1,0:T(8,128)(2,1)S(1)}, u32[]{:S(2)}) copy-start(bf16[128,256]{1,0:T(8,128)(2,1)S(1)} %fusion.2) | copy-start | bytes 196612
  55.3 2.5 %copy-start.25 = (bf16[256,256]{1,0:T(8,128)(2,1)S(1)}, bf16[256,256]{1,0:T(8,128)(2,1)}, u32[]{:S(2)}) copy-start(bf16[256,256]{1,0:T(8,128)(2,1)} %param.21) | copy-start | bytes 393220
  62.9 2.7 %copy-start.31 = (s32[1024]{0:T(1024)S(1)}, s32[1024]{0:T(1024)}, u32[]{:S(2)}) copy-start(s32[1024]{0:T(1024)} %get-tuple-element.44) | copy-start | bytes 12292
  63.6 9.3 %copy-start.6 = (bf16[128,256]{1,0:T(8,128)(2,1)S(1)}, bf16[128,256]{1,0:T(8,128)(2,1)}, u32[]{:S(2)}) copy-start(bf16[128,256]{1,0:T(8,128)(2,1)} %param.15) | copy-start | bytes 196612
  63.6 9.3 %copy-start.11 = (bf16[128,256]{1,0:T(8,128)(2,1)S(1)}, bf16[128,256]{1,0:T(8,128)(2,1)}, u32[]{:S(2)}) copy-start(bf16[128,256]{1,0:T(8,128)(2,1)} %copy-done.10) | copy-start | bytes 196612
  63.6 9.3 %copy-start.23 = (bf16[128,256]{1,0:T(8,128)(2,1)S(1)}, bf16[128,256]{1,0:T(8,128)(2,1)}, u32[]{:S(2)}) copy-start(bf16[128,256]{1,0:T(8,128)(2,1)} %copy-done.22) | copy-start | bytes 196612
  65.6 7.5 %copy-start.2 = (bf16[1024,256]{0,1:T(8,128)(2,1)S(1)}, bf16[1024,256]{0,1:T(8,128)(2,1)}, u32[]{:S(2)}) copy-start(bf16[1024,256]{0,1:T(8,128)(2,1)} %get-tuple-element.36) | copy-start | bytes 1572868
  68.0 7.3 %collective-permute-start.2 = (bf16[128,256]{1,0:T(8,128)(2,1)S(1)}, bf16[128,256]{1,0:T(8,128)(2,1)S(1)}, u32[]{:S(2)}, u32[]{:S(2)}) collective-permute-start(bf16[128,256]{1,0:T(8,128)(2,1)S(1)} %get-tuple-element.39), channel_id=1, source_target_pairs={{0,2},{2,4},{4,6},{6,8},{8,10},{10,12},{12,14},{14,16},{16,18},{18... | collective-permute-start | bytes 196616 | tf_op jit(solution)/shard_map/ppermute | solution.py:23
  71.6 6.2 %collective-permute-start.3 = (bf16[128,256]{1,0:T(8,128)(2,1)S(1)}, bf16[128,256]{1,0:T(8,128)(2,1)S(1)}, u32[]{:S(2)}, u32[]{:S(2)}) collective-permute-start(bf16[128,256]{1,0:T(8,128)(2,1)S(1)} %get-tuple-element.40), channel_id=1, source_target_pairs={{2,0},{4,2},{6,4},{8,6},{10,8},{12,10},{14,12},{16,14},{18,16},{20... | collective-permute-start | bytes 196616 | tf_op jit(solution)/shard_map/ppermute | solution.py:23
  73.2 6.2 %copy-start.4 = (f32[256,256]{1,0:T(8,128)S(1)}, f32[256,256]{1,0:T(8,128)}, u32[]{:S(2)}) copy-start(f32[256,256]{1,0:T(8,128)} %fusion.52) | copy-start | bytes 786436
  73.2 6.2 %copy-start.9 = (f32[768,256]{1,0:T(8,128)S(1)}, f32[768,256]{1,0:T(8,128)}, u32[]{:S(2)}) copy-start(f32[768,256]{1,0:T(8,128)} %fusion.10) | copy-start | bytes 2359300
  73.2 6.2 %copy-start.19 = (f32[256,256]{1,0:T(8,128)S(1)}, f32[256,256]{1,0:T(8,128)}, u32[]{:S(2)}) copy-start(f32[256,256]{1,0:T(8,128)} %fusion.41) | copy-start | bytes 786436
  73.2 6.2 %copy-start.30 = (f32[256]{0:T(256)S(1)}, f32[256]{0:T(256)}, u32[]{:S(2)}) copy-start(f32[256]{0:T(256)} %get-tuple-element.21) | copy-start | bytes 3076
  73.2 6.2 %copy-start.32 = (f32[256]{0:T(256)S(1)}, f32[256]{0:T(256)}, u32[]{:S(2)}) copy-start(f32[256]{0:T(256)} %get-tuple-element.24) | copy-start | bytes 3076
  75.2 68.4 %copy-start.8 = (f32[128,512]{1,0:T(8,128)S(1)}, f32[128,512]{1,0:T(8,128)}, u32[]{:S(2)}) copy-start(f32[128,512]{1,0:T(8,128)} %copy-done.7) | copy-start | bytes 786436
  75.2 68.4 %copy-start.21 = (bf16[128,256]{1,0:T(8,128)(2,1)S(1)}, bf16[128,256]{1,0:T(8,128)(2,1)}, u32[]{:S(2)}) copy-start(bf16[128,256]{1,0:T(8,128)(2,1)} %param.26) | copy-start | bytes 196612
  75.2 68.4 %reduce-scatter.6.cloned.1.call-start = ((), (), s32[]{:S(2)}) async-start(), calls=%async_computation.4 | async-start | bytes 196608 | tf_op jit(solution)/shard_map/reduce_scatter | solution.py:146
  (13 other events, 19.7 us)
Sparse Core Ops, SparseCore 0:
  31.1 10.1 reduce-scatter.3
  75.4 9.6 reduce-scatter.7
  87.3 8.7 reduce-scatter.5
where the time goes:
time: 152 us
  blocking collectives  68.4 us (45%)
  local copies, waits for them, and re-layouts  18 us (12%)
  matrix products  15.5 us (10%)
  between operations  15 us (10%)
  other arithmetic  12.3 us (8%)
  waiting for transfers between devices  11.5 us (8%)
  starting transfers between devices  11 us (7%)
    psum x1, blocking collectives, local(): lax.psum((d_w_edge_in, d_w_edge_out, d_gain_edge, d_w_node_in, d_w_node_o...  64.1 us
    reduce_scatter x1, waiting for transfers between devices, local(): lax.psum_scatter(partial_sums, 'rep', scatter_dimension=0, tiled=True)  9 us
    unnamed x81, local copies, waits for them, and re-layouts  5.84 us
    ppermute x2, starting transfers between devices, from_behind(): lax.ppermute(value, axis, [(source, source + steps) for source in range(f...  4.84 us
    ppermute x1, starting transfers between devices, padded(): before = lax.ppermute(last, axis, up)  4.74 us
    gather x2, local copies, waits for them, and re-layouts, local(): jnp.take(group_grad, recv_local, axis=0).astype(jnp.float32)  4.14 us
    gather x1, local copies, waits for them, and re-layouts, local(): jnp.take(grouped, recv_local, axis=0)  3.94 us
    gather x1, local copies, waits for them, and re-layouts, local(): jnp.take(extended, send_local, axis=0)  3.94 us
  transfers between devices with their start and end apart: 7, of which 2 were waited for; matrix products, arithmetic and copies ran while one was open for 8% of the time, Pallas kernels for 0%

commit v1 on v0

--- a/solution.py
+++ b/solution.py
@@ -2,6 +2,7 @@
 import jax.numpy as jnp
 from jax import lax
 from jax.sharding import PartitionSpec as P
+from jax.lax import psum
 
 
 def padded(x, sides, width):
@@ -151,9 +152,12 @@
         jnp.float32
     )
     d_nodes = (d_direct + edge_terms).astype(jnp.bfloat16)
-    summed = lax.psum(
-        (d_w_edge_in, d_w_edge_out, d_gain_edge, d_w_node_in, d_w_node_out, d_gain_node),
-        ("row", "rep"),
+    summed = psum(
+        psum(
+            (d_w_edge_in, d_w_edge_out, d_gain_edge, d_w_node_in, d_w_node_out, d_gain_node),
+            axis_name="rep",
+        ),
+        axis_name="row",
     )
     return (
         nodes_out,

time: 152 us -> 221 us (1.45)
  blocking collectives: 68.4 us -> 103 us
  waiting for transfers between devices: 11.5 us -> 43.8 us
    psum x1 -> x2, blocking collectives: 64.1 us -> 98.6 us  [the longest x1 96.1 us: local(): psum(psum((d_w_edge_in, d_w_edge_out, d_gain_edge, d_w_node_in, d_w_node_...]
    psum x0 -> x1, waiting for transfers between devices: none -> 23.7 us  [local(): psum((d_w_edge_in, d_w_edge_out, d_gain_edge, d_w_node_in, d_w_node_out,...]
    reduce_scatter x1, waiting for transfers between devices: 0.01 us -> 8.02 us  [local(): lax.psum_scatter(inner.astype(jnp.bfloat16), 'rep', scatter_dimension=0,...]
    unnamed x81 -> x105, local copies, waits for them, and re-layouts: 5.84 us -> 6.76 us
  transfers between devices with their start and end apart: 7 -> 8, of which waited for: 2 -> 4; matrix products, arithmetic and copies ran while one was open for 8% -> 8% of each run, Pallas kernels for 0% -> 0%
where the time goes in v1:
time: 221 us
  blocking collectives  103 us (47%)
  waiting for transfers between devices  43.8 us (20%)
  local copies, waits for them, and re-layouts  20.1 us (9%)
  matrix products  15.2 us (7%)
  between operations  15.1 us (7%)
  other arithmetic  12.3 us (6%)
  starting transfers between devices  11.2 us (5%)
    psum x1, blocking collectives, local(): psum(psum((d_w_edge_in, d_w_edge_out, d_gain_edge, d_w_node_in, d_w_node_...  96.1 us
    psum x1, waiting for transfers between devices, local(): psum((d_w_edge_in, d_w_edge_out, d_gain_edge, d_w_node_in, d_w_node_out,...  23.7 us
    reduce_scatter x1, waiting for transfers between devices, local(): lax.psum_scatter(partial_sums, 'rep', scatter_dimension=0, tiled=True)  8.99 us
    reduce_scatter x1, waiting for transfers between devices, local(): lax.psum_scatter(inner.astype(jnp.bfloat16), 'rep', scatter_dimension=0,...  8.02 us
    unnamed x105, local copies, waits for them, and re-layouts  6.76 us
    dot_general x4, matrix products, contract_rows(): lax.dot_general(left, right, (((0,), (0,)), ((), ())), preferred_element_...  5.26 us
    ppermute x2, starting transfers between devices, from_behind(): lax.ppermute(value, axis, [(source, source + steps) for source in range(f...  5 us
    ppermute x1, starting transfers between devices, padded(): before = lax.ppermute(last, axis, up)  4.74 us
  transfers between devices with their start and end apart: 8, of which 4 were waited for; matrix products, arithmetic and copies ran while one was open for 8% of the time, Pallas kernels for 0%

profile of v1, /device:TPU:0, one launch (start us, length us, event | category | flops | bytes accessed | tf_op | source)
XLA Modules:
  0.0 220.7 jit_solution(11098453348938133651)
XLA Ops:
  7.2 2.4 %all_gather.6 = bf16[256,256]{1,0:T(8,128)(2,1)S(1)} all-gather(bf16[128,256]{1,0:T(8,128)(2,1)} %param.15), channel_id=1, replica_groups=mesh['row'=16,'rep'=2] {'rep'}, dimensions={0}, use_global_device_ids=true | all-gather | bytes 196608 | tf_op jit(solution)/shard_map/all_gather | solution.py:75
  9.6 4.7 %collective-permute-start = (bf16[128,256]{1,0:T(8,128)(2,1)S(1)}, bf16[128,256]{1,0:T(8,128)(2,1)S(1)}, u32[]{:S(2)}, u32[]{:S(2)}) collective-permute-start(bf16[128,256]{1,0:T(8,128)(2,1)S(1)} %get-tuple-element.48), channel_id=1, source_target_pairs={{0,2},{2,4},{4,6},{6,8},{8,10},{10,12},{12,14},{14,16},{16,18},{18... | collective-permute-start | bytes 196616 | tf_op jit(solution)/shard_map/ppermute | solution.py:15
  14.4 1.3 collective-permute-start.1
  16.4 1.3 subtract_add_fusion
  19.6 3.9 %gather_fusion.1 = bf16[1024,256]{1,0:T(8,128)(2,1)S(1)} fusion(bf16[256,256]{1,0:T(8,128)(2,1)S(1)} %all_gather.6, s32[1024]{0:T(1024)S(1)} %fusion.36), kind=kCustom, calls=%fused_computation.clone | custom fusion | bytes 1052672 | tf_op jit(solution)/shard_map/jit(_take)/gather | solution.py:85
  23.9 3.9 %gather_fusion = bf16[1024,256]{1,0:T(8,128)(2,1)S(1)} fusion(bf16[512,256]{1,0:T(8,128)(2,1)S(1)} %pad_maximum_fusion.3, s32[1024]{0:T(1024)S(1)} %get-tuple-element.51), kind=kCustom, calls=%fused_computation.2 | custom fusion | bytes 1052672 | tf_op jit(solution)/shard_map/jit(_take)/gather | solution.py:85
  28.1 1.6 multiply_convert_fusion.1
  30.3 1.2 fusion.6
  31.6 1.0 copy.23
  32.8 9.0 %reduce-scatter.4.cloned.1.call-done = f32[128,256]{1,0:T(8,128)} async-done(((f32[256,256]{1,0:T(8,128)}), f32[128,256]{1,0:T(8,128)}) %reduce-scatter.4.cloned.1.call-update) | async-done | bytes 131088 | tf_op jit(solution)/shard_map/reduce_scatter | solution.py:99
  43.0 1.2 fusion.48
  44.4 2.1 fusion.30
  48.0 1.9 all_gather.7
  49.9 3.9 %gather_fusion.2 = bf16[1024,256]{1,0:T(8,128)(2,1)S(1)} fusion(bf16[256,256]{1,0:T(8,128)(2,1)S(1)} %all_gather.7, s32[1024]{0:T(1024)S(1)} %fusion.36), kind=kCustom, calls=%fused_computation.1.clone | custom fusion | bytes 1052672 | tf_op jit(solution)/shard_map/jit(_take)/gather | solution.py:120
  54.1 1.8 multiply_reduce_fusion
  58.6 1.5 fusion.10
  60.1 2.3 %fusion.49 = (bf16[1024,768]{1,0:T(8,128)(2,1)S(1)}, f32[1024,768]{1,0:T(8,128)}) fusion(bf16[1024,256]{1,0:T(8,128)(2,1)S(1)} %fusion.1, bf16[768,256]{1,0:T(8,128)(2,1)S(1)} %copy-done), kind=kOutput, calls=%fused_computation.99 | convolution fusion | flops 403439616 | bytes 5636096 | tf_op jit(solution)/shard_map/dot_general | solution.py:53
  63.4 1.3 fusion.50
  64.7 3.7 %collective-permute-start.2 = (bf16[128,256]{1,0:T(8,128)(2,1)S(1)}, bf16[128,256]{1,0:T(8,128)(2,1)S(1)}, u32[]{:S(2)}, u32[]{:S(2)}) collective-permute-start(bf16[128,256]{1,0:T(8,128)(2,1)S(1)} %get-tuple-element.45), channel_id=1, source_target_pairs={{0,2},{2,4},{4,6},{6,8},{8,10},{10,12},{12,14},{14,16},{16,18},{18... | collective-permute-start | bytes 196616 | tf_op jit(solution)/shard_map/ppermute | solution.py:24
  68.4 1.3 collective-permute-start.3
  69.8 1.6 fusion.41
  71.5 3.1 %collective-permute-done.3 = bf16[128,256]{1,0:T(8,128)(2,1)S(1)} collective-permute-done((bf16[128,256]{1,0:T(8,128)(2,1)S(1)}, bf16[128,256]{1,0:T(8,128)(2,1)S(1)}, u32[]{:S(2)}, u32[]{:S(2)}) %collective-permute-start.3) | collective-permute-done | bytes 65568 | tf_op jit(solution)/shard_map/ppermute | solution.py:24
  76.3 1.1 fusion.33
  77.4 1.0 fusion.52
  78.5 1.0 copy.27
  79.5 1.3 slice.68
  81.3 1.0 copy.28
  82.3 2.4 %all-reduce.1 = (f32[256]{0:T(256)S(1)}, f32[256]{0:T(256)S(1)}) all-reduce(f32[256]{0:T(256)S(1)} %copy-done.35, f32[256]{0:T(256)S(1)} %copy-done.37), channel_id=1, replica_groups=mesh['row'=16,'rep'=2] {'rep'}, use_global_device_ids=true, to_apply=%region_16.18 | all-reduce | flops 512 | bytes 4096 | tf_op jit(solution)/shard_map/psum | solution.py:156
  84.7 8.0 %reduce-scatter.6.cloned.1.call-done = bf16[128,256]{1,0:T(8,128)(2,1)} async-done(((bf16[256,256]{1,0:T(8,128)(2,1)}), bf16[128,256]{1,0:T(8,128)(2,1)}) %reduce-scatter.6.cloned.1.call-update) | async-done | bytes 65552 | tf_op jit(solution)/shard_map/reduce_scatter | solution.py:147
  92.8 1.5 fusion.29
  94.3 23.7 %all-reduce.6.cloned.1.call-done = (f32[768,256]{1,0:T(8,128)}, f32[256,256]{1,0:T(8,128)}, f32[512,256]{1,0:T(8,128)}, f32[256,256]{1,0:T(8,128)}) async-done(((f32[768,256]{1,0:T(8,128)}, f32[256,256]{1,0:T(8,128)}, f32[512,256]{1,0:T(8,128)}, f32[256,256]{1,0:T(8,128)}), (f32[768,256]{1,0:T(8,128)}, f32[256,256]{1,0:T(8,128)}, f32[512,256]{1,0:T(8,128)}, ...) | async-done | bytes 1835024 | tf_op jit(solution)/shard_map/psum | solution.py:156
  118.0 96.1 %all-reduce.7 = (bf16[768,256]{1,0:T(8,128)(2,1)}, bf16[256,256]{1,0:T(8,128)(2,1)}, f32[256]{0:T(256)}, bf16[512,256]{1,0:T(8,128)(2,1)}, bf16[256,256]{1,0:T(8,128)(2,1)}, /*index=5*/f32[256]{0:T(256)}) all-reduce(f32[768,256]{1,0:T(8,128)} %get-tuple-element.35, ...), channel_id=1, replica_groups=mesh['row'=16,'rep'=2] {'row'}, use_global_device_ids=true, to_apply=%region_12.14 | all-reduce | flops 459264 | bytes 2756608 | tf_op jit(solution)/shard_map/psum | solution.py:155
  (145 shorter events, 12.3 us)
Async XLA Ops:
  7.2 20.9 %copy-start = (bf16[768,256]{1,0:T(8,128)(2,1)S(1)}, bf16[768,256]{1,0:T(8,128)(2,1)}, u32[]{:S(2)}) copy-start(bf16[768,256]{1,0:T(8,128)(2,1)} %param.20) | copy-start | bytes 1179652
  7.2 34.6 %reduce-scatter.4.cloned.1.call-start = ((), (), s32[]{:S(2)}) async-start(), calls=%async_computation.3 | async-start | bytes 393216 | tf_op jit(solution)/shard_map/reduce_scatter | solution.py:99
  9.6 14.2 %collective-permute-start = (bf16[128,256]{1,0:T(8,128)(2,1)S(1)}, bf16[128,256]{1,0:T(8,128)(2,1)S(1)}, u32[]{:S(2)}, u32[]{:S(2)}) collective-permute-start(bf16[128,256]{1,0:T(8,128)(2,1)S(1)} %get-tuple-element.48), channel_id=1, source_target_pairs={{0,2},{2,4},{4,6},{6,8},{8,10},{10,12},{12,14},{14,16},{16,18},{18... | collective-permute-start | bytes 196616 | tf_op jit(solution)/shard_map/ppermute | solution.py:15
  14.4 9.4 %collective-permute-start.1 = (bf16[128,256]{1,0:T(8,128)(2,1)S(1)}, bf16[128,256]{1,0:T(8,128)(2,1)S(1)}, u32[]{:S(2)}, u32[]{:S(2)}) collective-permute-start(bf16[128,256]{1,0:T(8,128)(2,1)S(1)} %get-tuple-element.49), channel_id=1, source_target_pairs={{2,0},{4,2},{6,4},{8,6},{10,8},{12,10},{14,12},{16,14},{18,16},{20... | collective-permute-start | bytes 196616 | tf_op jit(solution)/shard_map/ppermute | solution.py:16
  19.0 4.5 %copy-start.33 = (pred[1024]{0:T(1024)(128)(4,1)}, pred[1024]{0:T(1024)(128)(4,1)S(1)}, u32[]{:S(2)}) copy-start(pred[1024]{0:T(1024)(128)(4,1)S(1)} %get-tuple-element.39) | copy-start | bytes 3076
  23.8 4.2 %copy-start.11 = (bf16[1024,256]{1,0:T(8,128)(2,1)}, bf16[1024,256]{1,0:T(8,128)(2,1)S(1)}, u32[]{:S(2)}) copy-start(bf16[1024,256]{1,0:T(8,128)(2,1)S(1)} %broadcast_select_fusion) | copy-start | bytes 1572868
  23.8 4.2 %copy-start.16 = (bf16[1024,256]{1,0:T(8,128)(2,1)S(1)}, bf16[1024,256]{1,0:T(8,128)(2,1)}, u32[]{:S(2)}) copy-start(bf16[1024,256]{1,0:T(8,128)(2,1)} %param.16) | copy-start | bytes 1572868
  31.5 11.2 %copy-start.4 = (bf16[512,256]{1,0:T(8,128)(2,1)S(1)}, bf16[512,256]{1,0:T(8,128)(2,1)}, u32[]{:S(2)}) copy-start(bf16[512,256]{1,0:T(8,128)(2,1)} %param.23) | copy-start | bytes 786436
  31.5 11.3 %copy-start.5 = (bf16[128,256]{1,0:T(8,128)(2,1)S(1)}, bf16[128,256]{1,0:T(8,128)(2,1)}, u32[]{:S(2)}) copy-start(bf16[128,256]{1,0:T(8,128)(2,1)} %param.15) | copy-start | bytes 196612
  31.5 53.2 %reduce-scatter.8.cloned.1.call-start = ((), (), s32[]{:S(2)}) async-start(), calls=%async_computation.5 | async-start | bytes 196608 | tf_op jit(solution)/shard_map/reduce_scatter | solution.py:149
  32.8 14.3 %copy-start.21 = (bf16[128,256]{1,0:T(8,128)(2,1)S(1)}, bf16[128,256]{1,0:T(8,128)(2,1)}, u32[]{:S(2)}) copy-start(bf16[128,256]{1,0:T(8,128)(2,1)} %param.26) | copy-start | bytes 196612
  32.8 14.3 %copy-start.42 = (f32[256]{0:T(256)S(1)}, f32[256]{0:T(256)}, u32[]{:S(2)}) copy-start(f32[256]{0:T(256)} %param.25) | copy-start | bytes 3076
  32.8 14.3 %copy-start.48 = (bf16[256,256]{1,0:T(8,128)(2,1)S(1)}, bf16[256,256]{1,0:T(8,128)(2,1)}, u32[]{:S(2)}) copy-start(bf16[256,256]{1,0:T(8,128)(2,1)} %param.24) | copy-start | bytes 393220
  42.8 3.8 %copy-start.9 = (bf16[128,256]{1,0:T(8,128)(2,1)}, bf16[128,256]{1,0:T(8,128)(2,1)S(1)}, u32[]{:S(2)}) copy-start(bf16[128,256]{1,0:T(8,128)(2,1)S(1)} %convert_element_type.98) | copy-start | bytes 196612
  43.0 4.7 %copy-start.26 = (f32[128,256]{1,0:T(8,128)}, f32[128,256]{1,0:T(8,128)S(1)}, u32[]{:S(2)}) copy-start(f32[128,256]{1,0:T(8,128)S(1)} %fusion.34) | copy-start | bytes 393220
  44.2 3.5 %copy-start.40 = (f32[128]{0:T(128)}, f32[128]{0:T(128)S(1)}, u32[]{:S(2)}) copy-start(f32[128]{0:T(128)S(1)} %broadcast_multiply_fusion.5) | copy-start | bytes 1540
  62.4 7.3 %copy-start.41 = (f32[128]{0:T(128)S(1)}, f32[128]{0:T(128)}, u32[]{:S(2)}) copy-start(f32[128]{0:T(128)} %copy-done.40) | copy-start | bytes 1540
  62.4 7.3 %copy-start.43 = (f32[256]{0:T(256)S(1)}, f32[256]{0:T(256)}, u32[]{:S(2)}) copy-start(f32[256]{0:T(256)} %param.25) | copy-start | bytes 3076
  62.4 7.3 %copy-start.45 = (f32[128]{0:T(128)S(1)}, f32[128]{0:T(128)}, u32[]{:S(2)}) copy-start(f32[128]{0:T(128)} %copy-done.44) | copy-start | bytes 1540
  63.4 6.3 %copy-start.20 = (f32[128,256]{1,0:T(8,128)S(1)}, f32[128,256]{1,0:T(8,128)}, u32[]{:S(2)}) copy-start(f32[128,256]{1,0:T(8,128)} %copy-done.19) | copy-start | bytes 393220
  63.4 6.3 %copy-start.22 = (bf16[128,256]{1,0:T(8,128)(2,1)S(1)}, bf16[128,256]{1,0:T(8,128)(2,1)}, u32[]{:S(2)}) copy-start(bf16[128,256]{1,0:T(8,128)(2,1)} %param.26) | copy-start | bytes 196612
  63.4 6.4 %copy-start.27 = (f32[128,256]{1,0:T(8,128)S(1)}, f32[128,256]{1,0:T(8,128)}, u32[]{:S(2)}) copy-start(f32[128,256]{1,0:T(8,128)} %copy-done.26) | copy-start | bytes 393220
  64.6 11.6 %copy-start.6 = (bf16[128,256]{1,0:T(8,128)(2,1)S(1)}, bf16[128,256]{1,0:T(8,128)(2,1)}, u32[]{:S(2)}) copy-start(bf16[128,256]{1,0:T(8,128)(2,1)} %param.15) | copy-start | bytes 196612
  64.7 11.6 %copy-start.10 = (bf16[128,256]{1,0:T(8,128)(2,1)S(1)}, bf16[128,256]{1,0:T(8,128)(2,1)}, u32[]{:S(2)}) copy-start(bf16[128,256]{1,0:T(8,128)(2,1)} %copy-done.9) | copy-start | bytes 196612
  64.7 11.7 %copy-start.25 = (bf16[128,256]{1,0:T(8,128)(2,1)S(1)}, bf16[128,256]{1,0:T(8,128)(2,1)}, u32[]{:S(2)}) copy-start(bf16[128,256]{1,0:T(8,128)(2,1)} %copy-done.24) | copy-start | bytes 196612
  64.7 12.7 %copy-start.2 = (bf16[1024,256]{0,1:T(8,128)(2,1)S(1)}, bf16[1024,256]{0,1:T(8,128)(2,1)}, u32[]{:S(2)}) copy-start(bf16[1024,256]{0,1:T(8,128)(2,1)} %copy-done.1) | copy-start | bytes 1572868
  64.7 6.8 %collective-permute-start.2 = (bf16[128,256]{1,0:T(8,128)(2,1)S(1)}, bf16[128,256]{1,0:T(8,128)(2,1)S(1)}, u32[]{:S(2)}, u32[]{:S(2)}) collective-permute-start(bf16[128,256]{1,0:T(8,128)(2,1)S(1)} %get-tuple-element.45), channel_id=1, source_target_pairs={{0,2},{2,4},{4,6},{6,8},{8,10},{10,12},{12,14},{14,16},{16,18},{18... | collective-permute-start | bytes 196616 | tf_op jit(solution)/shard_map/ppermute | solution.py:24
  68.4 6.2 %collective-permute-start.3 = (bf16[128,256]{1,0:T(8,128)(2,1)S(1)}, bf16[128,256]{1,0:T(8,128)(2,1)S(1)}, u32[]{:S(2)}, u32[]{:S(2)}) collective-permute-start(bf16[128,256]{1,0:T(8,128)(2,1)S(1)} %get-tuple-element.46), channel_id=1, source_target_pairs={{2,0},{4,2},{6,4},{8,6},{10,8},{12,10},{14,12},{16,14},{18,16},{20... | collective-permute-start | bytes 196616 | tf_op jit(solution)/shard_map/ppermute | solution.py:24
  71.4 21.4 %reduce-scatter.6.cloned.1.call-start = ((), (), s32[]{:S(2)}) async-start(), calls=%async_computation.4 | async-start | bytes 196608 | tf_op jit(solution)/shard_map/reduce_scatter | solution.py:147
  76.2 41.8 %all-reduce.6.cloned.1.call-start = ((), (), s32[]{:S(2)}) async-start(), calls=%async_computation.6 | async-start | bytes 3670016 | tf_op jit(solution)/shard_map/psum | solution.py:156
  81.1 11.7 %copy-start.8 = (f32[128,512]{1,0:T(8,128)S(1)}, f32[128,512]{1,0:T(8,128)}, u32[]{:S(2)}) copy-start(f32[128,512]{1,0:T(8,128)} %copy-done.7) | copy-start | bytes 786436
  81.1 11.6 %copy-start.23 = (bf16[128,256]{1,0:T(8,128)(2,1)S(1)}, bf16[128,256]{1,0:T(8,128)(2,1)}, u32[]{:S(2)}) copy-start(bf16[128,256]{1,0:T(8,128)(2,1)} %param.26) | copy-start | bytes 196612
  (26 other events, 39.5 us)
Sparse Core Ops, SparseCore 0:
  31.6 10.1 reduce-scatter.3
  71.5 9.6 reduce-scatter.7
  84.0 8.6 reduce-scatter.5
  95.8 22.1 all-reduce.5
